TPU v7x, 256 devices: a whole 4x4x8 slice. The times are simulated.
256 devices in a mesh: ctx: 16 (over x, y), head: 16 (over z, core).
Axes of the slice: x: 4, y: 4, z: 8, core: 2. Of those that a mesh axis runs over, the one named last changes fastest.
Arguments:
- tokens: bfloat16 [8192, 8192], P('ctx'), may hold values from -6 to 6
- w_zx: bfloat16 [8192, 2, 8192], P('ctx', None, 'head'), may hold values from -0.0625 to 0.0625
- zx_scale: float32 [2, 8192], P(None, 'head'), may hold values from 0.5 to 2
- w_bc: bfloat16 [8192, 8, 512], P('ctx'), may hold values from -0.0625 to 0.0625
- bc_scale: float32 [8, 512], replicated, may hold values from 0.5 to 2
- w_dt: bfloat16 [8192, 128], P('ctx', 'head'), may hold values from -0.0625 to 0.0625
- conv_x: float32 [5, 8192], P(None, 'head'), may hold values from -3 to 3
- conv_bc: float32 [5, 8, 512], replicated, may hold values from -3 to 3
- tail_x: bfloat16 [3, 8192], P(None, 'head'), may hold values from -6 to 6
- tail_bc: bfloat16 [3, 8, 512], replicated, may hold values from -6 to 6
- head_params: float32 [3, 128], P(None, 'head'), may hold values from -12 to 2, as said below
- init_state: float32 [128, 64, 256], P('head'), may hold values from -1.5 to 1.5
- norm_gain: float32 [8192], P('head'), may hold values from 0.5 to 1.5
Outputs:
- mixed: bfloat16 [8192, 8192], P('ctx', 'head')
Inputs may be any that keep to these rules, and one draw needn't show every extreme that they name: `head_params`: row 0 lies in -3.5 to -2.5 and row 2 in 0.5 to 1.5.
All inputs are finite; a program needn't handle non-finite values.
Results may differ from a plain program's by a relative error of at most 0.0052.
Values may be sent and summed in bfloat16 or wider, within the bound.
A program may use at most 256 MiB of HBM per device.

v0:
```python
import jax
import jax.numpy as jnp
from jax import lax
from jax.sharding import PartitionSpec as P

H = 128
P_SIZE = 64
N = 256
G = 8
K = 4


def passed_along(x, axis, by):
    length = lax.axis_size(axis)
    pairs = [(i, i + by) for i in range(length) if 0 <= i + by < length]
    return lax.ppermute(x, axis, pairs)


def prefix(part, axis, combine, identity):
    place = lax.axis_index(axis)
    gathered = jax.tree.map(lambda a: lax.all_gather(a, axis), part)
    state = jax.tree.map(lambda a, e: jnp.zeros_like(a) + jnp.asarray(e, a.dtype), part, identity)

    def one(lap, state):
        return combine(
            state, jax.tree.map(lambda a: lax.dynamic_index_in_dim(a, lap, 0, False), gathered)
        )

    return lax.fori_loop(0, place, one, state)


def conv_silu(values, before, taps):
    length = values.shape[0]
    padded = jnp.concatenate([before, values], 0).astype(jnp.float32)
    summed = taps[K]
    for tap_index in range(K):
        summed = summed + taps[tap_index] * padded[tap_index : tap_index + length]
    return jax.nn.silu(summed).astype(jnp.bfloat16)


def pick_group(values, group_index, axis_index):
    chosen = lax.dynamic_index_in_dim(values, group_index, axis_index, keepdims=False)
    return chosen


def body(
    tokens,
    w_zx,
    zx_scale,
    w_bc,
    bc_scale,
    w_dt,
    conv_x,
    conv_bc,
    tail_x,
    tail_bc,
    head_params,
    init_state,
    norm_gain,
):
    highest = lax.Precision.HIGHEST
    tok_rows = tokens.shape[0]
    local_heads = head_params.shape[1]
    channels = local_heads * P_SIZE
    per_group = H // G
    group_index = lax.axis_index("head") * local_heads // per_group
    bc_rows = pick_group(w_bc, group_index, 1)
    bc_scales = pick_group(bc_scale, group_index, 0)
    bc_taps = pick_group(conv_bc, group_index, 1)
    bc_tail = pick_group(tail_bc, group_index, 1)
    zx_rows = w_zx.reshape(w_zx.shape[0], 2 * channels)
    pieces = (
        lax.all_gather(zx_rows, "ctx", axis=0, tiled=True),
        lax.all_gather(bc_rows, "ctx", axis=0, tiled=True),
        lax.all_gather(w_dt, "ctx", axis=0, tiled=True),
    )
    zx_sum, bc_sum, step_sum = tuple(
        (jnp.dot(tokens, piece, preferred_element_type=jnp.float32) for piece in pieces)
    )
    zx_val = (zx_sum.reshape(tok_rows, 2, channels) * zx_scale).astype(jnp.bfloat16)
    gate = zx_val[:, 0]
    inner_in = zx_val[:, 1]
    bc_val = (bc_sum * bc_scales).astype(jnp.bfloat16)
    step_size = jax.nn.softplus(step_sum + head_params[0])
    edge = jnp.concatenate([inner_in[tok_rows - (K - 1) :], bc_val[tok_rows - (K - 1) :]], 1)
    arrived = passed_along(edge, "ctx", 1)
    previous = jnp.concatenate([tail_x, bc_tail], 1)
    arrived = jnp.where(lax.axis_index("ctx") == 0, previous, arrived)
    xconv = conv_silu(inner_in, arrived[:, :channels], conv_x)
    bconv = conv_silu(bc_val, arrived[:, channels:], bc_taps)
    b_part = bconv[:, :N]
    c_part = bconv[:, N:]
    x_heads = xconv.reshape(tok_rows, local_heads, P_SIZE).astype(jnp.float32)
    rate = -jnp.exp(head_params[1]) * step_size
    cumul = jnp.cumsum(rate, 0)
    cumul_t = cumul.T
    order = jnp.arange(tok_rows)
    lower = order[:, None] >= order[None, :]
    spread = cumul_t[:, :, None] - cumul_t[:, None, :]
    decay = jnp.where(lower[None], jnp.exp(jnp.minimum(spread, 0.0)), 0.0)
    scores = jnp.dot(c_part, b_part.T, preferred_element_type=jnp.float32)
    weights = decay * scores[None] * step_size.T[:, None, :]
    inner = jnp.einsum("hts,shp->thp", weights, x_heads, precision=highest)
    log_total = cumul[tok_rows - 1]
    fade = jnp.exp(log_total[None, :] - cumul) * step_size
    local_state = jnp.einsum(
        "sh,shp,sn->hpn", fade, x_heads, b_part.astype(jnp.float32), precision=highest
    )

    def combine(earlier, later):
        return (earlier[0] + later[0], jnp.exp(later[0])[:, None, None] * earlier[1] + later[1])

    before_log, before_state = prefix(
        (log_total, local_state),
        "ctx",
        combine,
        (jnp.zeros_like(log_total), jnp.zeros_like(local_state)),
    )
    incoming = jnp.exp(before_log)[:, None, None] * init_state + before_state
    carried = (
        jnp.einsum("tn,hpn->thp", c_part.astype(jnp.float32), incoming, precision=highest)
        * jnp.exp(cumul)[:, :, None]
    )
    y_val = inner + carried + head_params[2][None, :, None] * x_heads
    gated = y_val.reshape(tok_rows, channels) * jax.nn.silu(gate.astype(jnp.float32))
    squares = jnp.sum(gated * gated, axis=1)
    slot_hits = (jnp.arange(G) == group_index).astype(jnp.float32)
    placed = slot_hits[:, None] * squares[None, :]
    group_sums = lax.psum(placed, "head")
    totals = lax.dynamic_index_in_dim(group_sums, group_index, 0, keepdims=False)
    meansq = totals / (per_group * P_SIZE)
    mixed = gated * lax.rsqrt(meansq + 1e-05)[:, None] * norm_gain
    return mixed.astype(jnp.bfloat16)


def solution(mesh):
    return jax.shard_map(
        body,
        mesh=mesh,
        in_specs=(
            P("ctx", None),
            P("ctx", None, "head"),
            P(None, "head"),
            P("ctx", None, None),
            P(),
            P("ctx", "head"),
            P(None, "head"),
            P(),
            P(None, "head"),
            P(),
            P(None, "head"),
            P("head", None, None),
            P("head"),
        ),
        out_specs=P("ctx", "head"),
        check_vma=False,
    )
```

profile of v0, /device:TPU:30, one launch (start us, length us, event | category | flops | bytes accessed | tf_op | source)
XLA Modules:
  0.0 391.0 jit_solution(2558766528780283261)
XLA Ops:
  6.5 3.3 constant_dynamic-slice_fusion.8
  9.8 0.9 copy.38
  10.7 0.0 all-gather.9.cloned.1.call-update
  10.8 0.0 all-gather.7.cloned.1.call-start
  10.8 2.5 copy.40
  13.4 0.0 all-gather.7.cloned.1.call-update
  13.4 0.0 all-gather.11.cloned.1.call-start
  13.5 21.8 %all_gather.20 = bf16[8192,8]{0,1:T(8,128)(2,1)S(1)} all-gather(bf16[512,8]{0,1:T(8,128)(2,1)} %param.20), channel_id=1, replica_groups=mesh['ctx'=16,'head'=16] {'ctx'}, dimensions={0}, use_global_device_ids=true | all-gather | bytes 139264 | tf_op jit(solution)/shard_map/all_gather | solution.py:75
  35.3 0.8 slice_bitcast_fusion.2
  36.1 5.7 %convolution_add_fusion = f32[512,8]{0,1:T(8,128)S(1)} fusion(bf16[512,8192]{1,0:T(8,128)(2,1)} %param.15, bf16[8192,8]{0,1:T(8,128)(2,1)S(1)} %all_gather.20, f32[8]{0:T(128)S(1)} %get-tuple-element.93), kind=kOutput, calls=%fused_computation.30 | convolution fusion | flops 67112960 | bytes 8536096 | tf_op jit(solution)/shard_map/dot_general | solution.py:78
  41.8 0.1 multiply_bitcast_fusion
  41.9 1.1 reduce-window.6
  43.0 0.2 slice_reduce_fusion
  43.2 0.7 constant_dynamic-slice_fusion.7
  44.0 0.1 fusion.66
  44.0 0.2 slice_reduce_fusion.1
  44.2 0.8 constant_dynamic-slice_fusion.4
  45.0 0.1 fusion.57
  45.1 42.5 %all-gather.9.cloned.1.call-done = bf16[8192,1,512]{2,0,1:T(8,128)(2,1)} async-done(((bf16[512,1,512]{2,0,1:T(8,128)(2,1)}), bf16[8192,1,512]{2,0,1:T(8,128)(2,1)}) %all-gather.9.cloned.1.call-update) | async-done | bytes 8388624 | tf_op jit(solution)/shard_map/all_gather | solution.py:74
  87.6 10.2 %fusion.27 = bf16[512,512]{1,0:T(8,128)(2,1)S(1)} fusion(bf16[512,8192]{1,0:T(8,128)(2,1)} %param.15, bf16[8192,1,512]{2,0,1:T(8,128)(2,1)} %all-gather.9.cloned.1.call-done, f32[512]{0:T(512)S(1)} %bitcast.142), kind=kOutput, calls=%fused_computation.29 | convolution fusion | flops 4295491584 | bytes 17303552 | tf_op jit(solution)/shard_map/dot_general | solution.py:78
  97.9 0.0 copy-start.4
  97.9 0.8 copy-done.4
  98.7 107.3 %all-gather.7.cloned.1.call-done = bf16[8192,1024]{1,0:T(8,128)(2,1)} async-done(((bf16[512,1024]{1,0:T(8,128)(2,1)}), bf16[8192,1024]{1,0:T(8,128)(2,1)}) %all-gather.7.cloned.1.call-update) | async-done | bytes 16777232 | tf_op jit(solution)/shard_map/all_gather | solution.py:73
  206.0 14.3 %fusion.69 = f32[512,1024]{1,0:T(8,128)S(1)} fusion(bf16[512,8192]{1,0:T(8,128)(2,1)} %param.15, bf16[8192,1024]{1,0:T(8,128)(2,1)} %all-gather.7.cloned.1.call-done), kind=kOutput, calls=%fused_computation.115 | convolution fusion | flops 8589934592 | bytes 27262976 | tf_op jit(solution)/shard_map/dot_general | solution.py:78
  220.4 0.3 fusion.15
  220.7 1.5 collective-permute-start
  222.2 0.2 slice_convert_fusion
  222.4 3.9 collective-permute-done
  226.3 0.2 maximum_convert_fusion
  226.5 1.5 multiply_convert_fusion.1
  228.0 2.1 copy.31
  230.0 0.7 multiply_convert_fusion
  230.7 0.8 copy-done.1
  231.5 2.5 fusion.30
  234.0 0.0 all-gather.11.cloned.1.call-update
  234.0 21.3 %all-gather.2 = f32[16,1,8]{2,1,0:T(1,128)S(1)} all-gather(f32[1,1,8]{2,1,0:T(1,128)S(1)} %bitcast.141), channel_id=1, replica_groups=mesh['ctx'=16,'head'=16] {'ctx'}, dimensions={0}, use_global_device_ids=true | all-gather | bytes 544 | tf_op jit(solution)/shard_map/all_gather | solution.py:21
  255.3 0.1 iota_compare_fusion
  255.4 0.1 add_bitcast_fusion.1
  255.5 1.4 copy.35
  256.9 1.4 fusion.53
  258.2 8.7 %fusion.16 = f32[512,8,64]{0,2,1:T(8,128)} fusion(bf16[512,8,64]{0,2,1:T(8,128)(2,1)} %bitcast.122, f32[8,512]{1,0:T(8,128)S(1)} %get-tuple-element.83, f32[512,512]{1,0:T(8,128)S(1)} %fusion.53, f32[8,512]{1,0:T(8,128)S(1)} %add_bitcast_fusion.1, pred[512,512]{1,0:T(8,128)(4,1)S(1)} %iota_compare_fusion), kind=kOutput, calls=%fused_computation.21 | convolution fusion | flops 1621098496 | bytes 2916352 | tf_op jit(solution)/shard_map/hts,shp->thp/dot_general | solution.py:103
  266.9 44.0 %all-gather.11.cloned.1.call-done = f32[128,64,256]{2,1,0:T(8,128)} async-done(((f32[8,64,256]{2,1,0:T(8,128)}), f32[128,64,256]{2,1,0:T(8,128)}) %all-gather.11.cloned.1.call-update) | async-done | bytes 8388624 | tf_op jit(solution)/shard_map/all_gather | solution.py:21
  311.0 0.0 copy-start.9
  311.0 18.8 %while.12 = (s32[]{:T(128)}, f32[8]{0:T(128)S(1)}, f32[8,64,256]{2,1,0:T(8,128)S(1)}, s32[]{:T(128)}, f32[16,8]{1,0:T(8,128)S(1)}, /*index=5*/f32[16,8,64,256]{3,2,1,0:T(8,128)}, s32[]{:T(128)}, s32[]{:T(128)}, s32[]{:T(128)}) while((s32[]{:T(128)}, f32[8]{0:T(128)S(1)}, f32[8,64,256]{2,1,0:T(8,128)S(1)}, s32[]{:T(128)}, ...), condition=%wide.region_3.4_spmd, body=%wide.region_2.3_spmd.sunk | while | flops 262157 | bytes 1573167 | solution.py:29
  311.1 1.2 bitcast_add_fusion.3
  312.3 1.2 bitcast_add_fusion.3
  313.6 1.2 bitcast_add_fusion.3
  314.8 1.2 bitcast_add_fusion.3
  316.1 1.2 bitcast_add_fusion.3
  317.3 1.2 bitcast_add_fusion.3
  318.6 1.2 bitcast_add_fusion.3
  319.8 1.2 bitcast_add_fusion.3
  321.1 1.2 bitcast_add_fusion.3
  322.3 1.2 bitcast_add_fusion.3
  323.6 1.2 bitcast_add_fusion.3
  324.9 1.2 bitcast_add_fusion.3
  326.1 1.2 bitcast_add_fusion.3
  327.4 1.2 bitcast_add_fusion.3
  328.6 1.2 bitcast_add_fusion.3
  329.9 3.6 multiply_reduce_fusion
  333.5 1.6 copy.34
  335.1 0.1 broadcast_multiply_fusion
  335.1 48.1 %psum.7 = f32[8,512]{1,0:T(8,128)S(1)} all-reduce(f32[8,512]{1,0:T(8,128)S(1)} %broadcast_multiply_fusion), channel_id=1, replica_groups=mesh['ctx'=16,'head'=16] {'head'}, use_global_device_ids=true, to_apply=%region_5.6 | all-reduce | flops 4096 | bytes 32768 | tf_op jit(solution)/shard_map/psum | solution.py:129
  383.3 1.2 fusion.45
  (47 shorter events, 0.5 us)
Async XLA Ops:
  6.5 6.9 %copy-start = (bf16[3,8,512]{2,1,0:T(8,128)(2,1)S(1)}, bf16[3,8,512]{2,1,0:T(8,128)(2,1)}, u32[]{:S(2)}) copy-start(bf16[3,8,512]{2,1,0:T(8,128)(2,1)} %param.24) | copy-start | bytes 73732
  6.5 38.5 %copy-start.6 = (f32[5,512]{1,0:T(8,128)S(1)}, f32[5,512]{1,0:T(8,128)}, u32[]{:S(2)}) copy-start(f32[5,512]{1,0:T(8,128)} %param.21) | copy-start | bytes 30724
  6.5 81.1 %all-gather.9.cloned.1.call-start = ((), (), s32[]{:S(2)}) async-start(), calls=%async_computation.1 | async-start | bytes 8912896 | tf_op jit(solution)/shard_map/all_gather | solution.py:74
  10.8 195.3 %all-gather.7.cloned.1.call-start = ((), (), s32[]{:S(2)}) async-start(), calls=%async_computation | async-start | bytes 17825792 | tf_op jit(solution)/shard_map/all_gather | solution.py:73
  13.4 297.6 %all-gather.11.cloned.1.call-start = ((), (), s32[]{:S(2)}) async-start(), calls=%async_computation.2 | async-start | bytes 8912896 | tf_op jit(solution)/shard_map/all_gather | solution.py:21
  97.9 0.8 copy-start.4
  98.7 121.7 %copy-start.7 = (f32[2,512]{1,0:T(2,128)S(1)}, f32[2,512]{1,0:T(2,128)}, u32[]{:S(2)}) copy-start(f32[2,512]{1,0:T(2,128)} %param.17) | copy-start | bytes 12292
  98.7 127.6 %copy-start.8 = (bf16[3,512]{1,0:T(4,128)(2,1)S(1)}, bf16[3,512]{1,0:T(4,128)(2,1)}, u32[]{:S(2)}) copy-start(bf16[3,512]{1,0:T(4,128)(2,1)} %param.23) | copy-start | bytes 9220
  206.0 20.2 %copy-start.5 = (bf16[512,512]{1,0:T(8,128)(2,1)S(1)}, bf16[512,512]{1,0:T(8,128)(2,1)}, u32[]{:S(2)}) copy-start(bf16[512,512]{1,0:T(8,128)(2,1)} %copy-done.4) | copy-start | bytes 1572868
  220.7 5.5 %collective-permute-start = (bf16[3,1024]{1,0:T(4,128)(2,1)S(1)}, bf16[3,1024]{1,0:T(4,128)(2,1)S(1)}, u32[]{:S(2)}, u32[]{:S(2)}) collective-permute-start(bf16[3,1024]{1,0:T(4,128)(2,1)S(1)} %pad_maximum_fusion), channel_id=1, source_target_pairs={{0,16},{16,32},{32,48},{48,64},{64,80},{80,96},{96,112},{112,128},... | collective-permute-start | bytes 18440 | tf_op jit(solution)/shard_map/ppermute | solution.py:16
  230.7 0.8 copy-start.1
  258.2 71.6 %copy-start.2 = (bf16[512,512]{1,0:T(8,128)(2,1)S(1)}, bf16[512,512]{1,0:T(8,128)(2,1)}, u32[]{:S(2)}) copy-start(bf16[512,512]{1,0:T(8,128)(2,1)} %copy-done.1) | copy-start | bytes 1572868
  258.2 71.6 %copy-start.3 = (bf16[512,512]{0,1:T(8,128)(2,1)S(1)}, bf16[512,512]{0,1:T(8,128)(2,1)}, u32[]{:S(2)}) copy-start(bf16[512,512]{0,1:T(8,128)(2,1)} %copy.31) | copy-start | bytes 1572868
  311.0 72.3 %copy-start.9 = (f32[512]{0:T(512)S(1)}, f32[512]{0:T(512)}, u32[]{:S(2)}) copy-start(f32[512]{0:T(512)} %param.27) | copy-start | bytes 6148
Sparse Core Ops, SparseCore 0:
  10.9 76.6 all-gather.8
  90.1 115.9 all-gather.6
  234.2 76.7 all-gather.10
where the time goes:
time: 392 us; the launch traced here: 391 us
  waiting for transfers between devices  198 us (51%)
  blocking collectives  91.2 us (23%)
  matrix products  46.4 us (12%)
  other arithmetic  24.9 us (6%)
  local copies, waits for them, and re-layouts  15.4 us (4%)
  between operations  13.4 us (3%)
    all_gather x1, waiting for transfers between devices, body(): lax.all_gather(zx_rows, 'ctx', axis=0, tiled=True)  107 us
    psum x1, blocking collectives, body(): group_sums = lax.psum(placed, 'head')  48.1 us
    all_gather x1, waiting for transfers between devices, prefix(): gathered = jax.tree.map(lambda a: lax.all_gather(a, axis), part)  44 us
    all_gather x1, waiting for transfers between devices, body(): lax.all_gather(bc_rows, 'ctx', axis=0, tiled=True)  42.5 us
    dot_general x3, matrix products, body(): jnp.dot(tokens, piece, preferred_element_type=jnp.float32)  30.3 us
    all_gather x1, blocking collectives, body(): lax.all_gather(w_dt, 'ctx', axis=0, tiled=True)  21.8 us
    all_gather x1, blocking collectives, prefix(): gathered = jax.tree.map(lambda a: lax.all_gather(a, axis), part)  21.3 us
    add x15, other arithmetic, combine(): jnp.exp(later[0])[:, None, None] * earlier[1] + later[1]  18.1 us
  transfers between devices with their start and end apart: 4, of which 4 were waited for; matrix products, arithmetic and copies ran while one was open for 9% of the time, Pallas kernels for 0%

commit v1 on v0

--- a/solution.py
+++ b/solution.py
@@ -70,7 +70,9 @@
     bc_tail = pick_group(tail_bc, group_index, 1)
     zx_rows = w_zx.reshape(w_zx.shape[0], 2 * channels)
     pieces = (
-        lax.all_gather(zx_rows, "ctx", axis=0, tiled=True),
+        jnp.concatenate(
+            lax.all_to_all(jnp.stack([zx_rows] * lax.axis_size("ctx")), "ctx", 0, 0), axis=0
+        ),
         lax.all_gather(bc_rows, "ctx", axis=0, tiled=True),
         lax.all_gather(w_dt, "ctx", axis=0, tiled=True),
     )

time: 392 us -> 599 us (1.53)
  blocking collectives: 91.2 us -> 397 us
  waiting for transfers between devices: 198 us -> 49.8 us
  local copies, waits for them, and re-layouts: 15.4 us -> 60.6 us
  starting transfers between devices: 1.56 us -> 8.77 us
    all_gather x1, blocking collectives: 21.8 us -> 330 us  [body(): lax.all_gather(w_dt, 'ctx', axis=0, tiled=True)]
    all_gather x1 -> x0, waiting for transfers between devices: 107 us -> none  [body(): lax.all_gather(zx_rows, 'ctx', axis=0, tiled=True)]
    all_gather x1, waiting for transfers between devices: 42.5 us -> 0.01 us  [body(): lax.all_gather(bc_rows, 'ctx', axis=0, tiled=True)]
    all_to_all x0 -> x1, local copies, waits for them, and re-layouts: none -> 21.7 us  [body(): lax.all_to_all(jnp.stack([zx_rows] * lax.axis_size('ctx')), 'ctx', 0, 0)]
    dot_general x0 -> x1, local copies, waits for them, and re-layouts: none -> 21.3 us  [body(): jnp.dot(tokens, piece, preferred_element_type=jnp.float32)]
    another operation x2 -> x4, local copies, waits for them, and re-layouts: 0.01 us -> 8.39 us  [the longest x2 8.38 us: body(): jnp.stack([zx_rows] * lax.axis_size('ctx'))]
    all_to_all x0 -> x1, starting transfers between devices: none -> 7.22 us  [body(): lax.all_to_all(jnp.stack([zx_rows] * lax.axis_size('ctx')), 'ctx', 0, 0)]
  transfers between devices with their start and end apart: 4 -> 4, of which waited for: 4 -> 2; matrix products, arithmetic and copies ran while one was open for 9% -> 11% of each run, Pallas kernels for 0% -> 0%
where the time goes in v1:
time: 599 us; the launch traced here: 597 us
  blocking collectives  397 us (66%)
  local copies, waits for them, and re-layouts  60.6 us (10%)
  waiting for transfers between devices  49.8 us (8%)
  matrix products  43.8 us (7%)
  other arithmetic  23.1 us (4%)
  between operations  13.7 us (2%)
  starting transfers between devices  8.77 us (1%)
    all_gather x1, blocking collectives, body(): lax.all_gather(w_dt, 'ctx', axis=0, tiled=True)  330 us
    psum x1, blocking collectives, body(): group_sums = lax.psum(placed, 'head')  48.1 us
    all_gather x1, waiting for transfers between devices, prefix(): gathered = jax.tree.map(lambda a: lax.all_gather(a, axis), part)  45.9 us
    dot_general x3, matrix products, body(): jnp.dot(tokens, piece, preferred_element_type=jnp.float32)  30.8 us
    all_to_all x1, local copies, waits for them, and re-layouts, body(): lax.all_to_all(jnp.stack([zx_rows] * lax.axis_size('ctx')), 'ctx', 0, 0)  21.7 us
    dot_general x1, local copies, waits for them, and re-layouts, body(): jnp.dot(tokens, piece, preferred_element_type=jnp.float32)  21.3 us
    all_gather x1, blocking collectives, prefix(): gathered = jax.tree.map(lambda a: lax.all_gather(a, axis), part)  18.7 us
    add x15, other arithmetic, combine(): jnp.exp(later[0])[:, None, None] * earlier[1] + later[1]  18.2 us
  transfers between devices with their start and end apart: 4, of which 2 were waited for; matrix products, arithmetic and copies ran while one was open for 11% of the time, Pallas kernels for 0%

profile of v1, /device:TPU:30, one launch (start us, length us, event | category | flops | bytes accessed | tf_op | source)
XLA Modules:
  0.0 597.1 jit_solution(2945144455716168796)
XLA Ops:
  6.5 2.5 copy.45
  9.0 5.9 stack.3
  14.9 7.2 %all-to-all-start = ((bf16[16,512,1024]{1,2,0:T(8,128)(2,1)}), bf16[16,512,1024]{1,2,0:T(8,128)(2,1)}, u32[]{:S(2)}, u32[]{:S(2)}) async-start(bf16[16,512,1024]{1,2,0:T(8,128)(2,1)} %stack.3), calls=%async_computation | async-start | bytes 33554432 | tf_op jit(solution)/shard_map/all_to_all | solution.py:74
  22.2 0.0 all-gather.6.cloned.1.call-start
  22.2 3.3 constant_dynamic-slice_fusion.8
  25.5 0.9 copy.48
  26.4 0.0 all-gather.6.cloned.1.call-update
  26.4 0.0 all-gather.8.cloned.1.call-start
  26.5 0.0 copy-done
  26.6 330.0 %all_gather.16 = bf16[8192,8]{0,1:T(8,128)(2,1)S(1)} all-gather(bf16[512,8]{0,1:T(8,128)(2,1)S(1)} %copy-done.4), channel_id=1, replica_groups=mesh['ctx'=16,'head'=16] {'ctx'}, dimensions={0}, use_global_device_ids=true | all-gather | bytes 139264 | tf_op jit(solution)/shard_map/all_gather | solution.py:77
  356.6 5.6 convolution_add_fusion
  362.2 0.1 multiply_bitcast_fusion
  362.3 1.1 reduce-window.6
  363.4 0.2 slice_reduce_fusion
  363.6 0.7 constant_dynamic-slice_fusion.7
  364.4 0.1 fusion.69
  364.4 0.2 slice_reduce_fusion.1
  364.6 0.8 constant_dynamic-slice_fusion.4
  365.5 0.1 fusion.60
  365.5 0.0 all-to-all-done
  365.5 21.7 %copy.37 = bf16[16,512,1024]{2,1,0:T(8,128)(2,1)} copy(bf16[16,512,1024]{1,2,0:T(8,128)(2,1)} %all-to-all-done) | data formatting | bytes 33554432 | tf_op jit(solution)/shard_map/all_to_all | solution.py:74
  387.2 21.3 %copy.38 = bf16[1024,8192]{1,0:T(8,128)(2,1)} copy(bf16[1024,8192]{0,1:T(8,128)(2,1)} %bitcast.121) | data formatting | bytes 33554432 | tf_op jit(solution)/shard_map/dot_general | solution.py:80
  408.5 10.3 %fusion.30 = bf16[512,512]{1,0:T(8,128)(2,1)S(1)} fusion(bf16[512,8192]{1,0:T(8,128)(2,1)} %param.15, bf16[8192,1,512]{2,0,1:T(8,128)(2,1)} %all-gather.6.cloned.1.call-done, f32[512]{0:T(512)S(1)} %bitcast.144), kind=kOutput, calls=%fused_computation.30 | convolution fusion | flops 4295491584 | bytes 17303552 | tf_op jit(solution)/shard_map/dot_general | solution.py:80
  418.8 0.0 copy-start.6
  418.8 14.9 %multiply_convert_fusion = bf16[512,2,512]{2,0,1:T(8,128)(2,1)S(1)} fusion(bf16[2,512,8192]{2,1,0:T(8,128)(2,1)} %bitcast.122, bf16[512,8192]{1,0:T(8,128)(2,1)} %param.15, f32[2,512]{1,0:T(2,128)S(1)} %copy-done.9), kind=kOutput, calls=%fused_computation.21 | convolution fusion | flops 8590983168 | bytes 26218496 | tf_op jit(solution)/shard_map/dot_general | solution.py:80
  433.8 1.5 collective-permute-start
  435.3 0.2 slice_convert_fusion
  435.4 3.9 collective-permute-done
  439.4 0.2 maximum_convert_fusion
  439.6 0.7 multiply_convert_fusion.2
  440.3 0.2 copy.40
  440.5 0.7 multiply_convert_fusion.1
  441.2 1.5 fusion.33
  442.7 0.0 all-gather.8.cloned.1.call-update
  442.7 18.7 %all-gather.2 = f32[16,1,8]{2,1,0:T(1,128)S(1)} all-gather(f32[1,1,8]{2,1,0:T(1,128)S(1)} %bitcast.143), channel_id=1, replica_groups=mesh['ctx'=16,'head'=16] {'ctx'}, dimensions={0}, use_global_device_ids=true | all-gather | bytes 544 | tf_op jit(solution)/shard_map/all_gather | solution.py:21
  461.4 0.1 iota_compare_fusion
  461.5 0.1 add_bitcast_fusion.1
  461.6 1.3 copy.44
  462.9 0.3 fusion.56
  463.2 7.6 %fusion.19 = f32[512,8,64]{0,2,1:T(8,128)} fusion(bf16[512,8,64]{0,2,1:T(8,128)(2,1)S(1)} %bitcast.125, f32[8,512]{1,0:T(8,128)S(1)} %get-tuple-element.89, f32[512,512]{1,0:T(8,128)S(1)} %fusion.56, f32[8,512]{1,0:T(8,128)S(1)} %add_bitcast_fusion.1, pred[512,512]{1,0:T(8,128)(4,1)S(1)} %iota_compare_fusion), kind=kOutput, calls=%fused_computation.22 | convolution fusion | flops 1621098496 | bytes 2916352 | tf_op jit(solution)/shard_map/hts,shp->thp/dot_general | solution.py:105
  470.7 45.9 %all-gather.8.cloned.1.call-done = f32[128,64,256]{2,1,0:T(8,128)} async-done(((f32[8,64,256]{2,1,0:T(8,128)}), f32[128,64,256]{2,1,0:T(8,128)}) %all-gather.8.cloned.1.call-update) | async-done | bytes 8388624 | tf_op jit(solution)/shard_map/all_gather | solution.py:21
  516.7 0.0 copy-start.1
  516.7 0.0 copy-start.7
  516.7 18.9 %while.12 = (s32[]{:T(128)}, f32[8]{0:T(128)S(1)}, f32[8,64,256]{2,1,0:T(8,128)S(1)}, s32[]{:T(128)}, f32[16,8]{1,0:T(8,128)S(1)}, /*index=5*/f32[16,8,64,256]{3,2,1,0:T(8,128)}, s32[]{:T(128)}, s32[]{:T(128)}, s32[]{:T(128)}) while((s32[]{:T(128)}, f32[8]{0:T(128)S(1)}, f32[8,64,256]{2,1,0:T(8,128)S(1)}, s32[]{:T(128)}, ...), condition=%wide.region_3.4_spmd, body=%wide.region_2.3_spmd.sunk | while | flops 262157 | bytes 1573167 | solution.py:29
  516.7 1.3 bitcast_add_fusion.3
  518.1 1.2 bitcast_add_fusion.3
  519.3 1.2 bitcast_add_fusion.3
  520.6 1.2 bitcast_add_fusion.3
  521.8 1.2 bitcast_add_fusion.3
  523.1 1.2 bitcast_add_fusion.3
  524.3 1.2 bitcast_add_fusion.3
  525.6 1.2 bitcast_add_fusion.3
  526.8 1.2 bitcast_add_fusion.3
  528.1 1.2 bitcast_add_fusion.3
  529.4 1.2 bitcast_add_fusion.3
  530.6 1.2 bitcast_add_fusion.3
  531.9 1.2 bitcast_add_fusion.3
  533.1 1.2 bitcast_add_fusion.3
  534.4 1.2 bitcast_add_fusion.3
  535.6 3.7 multiply_reduce_fusion
  539.3 1.6 copy.43
  540.9 0.1 broadcast_multiply_fusion
  540.9 48.1 %psum.7 = f32[8,512]{1,0:T(8,128)S(1)} all-reduce(f32[8,512]{1,0:T(8,128)S(1)} %broadcast_multiply_fusion), channel_id=1, replica_groups=mesh['ctx'=16,'head'=16] {'head'}, use_global_device_ids=true, to_apply=%region_5.6 | all-reduce | flops 4096 | bytes 32768 | tf_op jit(solution)/shard_map/psum | solution.py:131
  589.1 1.2 fusion.48
  (48 shorter events, 0.5 us)
Async XLA Ops:
  6.5 20.0 %copy-start = (bf16[3,8,512]{2,1,0:T(8,128)(2,1)S(1)}, bf16[3,8,512]{2,1,0:T(8,128)(2,1)}, u32[]{:S(2)}) copy-start(bf16[3,8,512]{2,1,0:T(8,128)(2,1)} %param.24) | copy-start | bytes 73732
  14.9 11.6 %copy-start.4 = (bf16[512,8]{0,1:T(8,128)(2,1)S(1)}, bf16[512,8]{0,1:T(8,128)(2,1)}, u32[]{:S(2)}) copy-start(bf16[512,8]{0,1:T(8,128)(2,1)} %param.20) | copy-start | bytes 24580
  14.9 341.6 %copy-start.8 = (f32[3,8]{1,0:T(4,128)S(1)}, f32[3,8]{1,0:T(4,128)}, u32[]{:S(2)}) copy-start(f32[3,8]{1,0:T(4,128)} %param.25) | copy-start | bytes 292
  14.9 350.6 %all-to-all-start = ((bf16[16,512,1024]{1,2,0:T(8,128)(2,1)}), bf16[16,512,1024]{1,2,0:T(8,128)(2,1)}, u32[]{:S(2)}, u32[]{:S(2)}) async-start(bf16[16,512,1024]{1,2,0:T(8,128)(2,1)} %stack.3), calls=%async_computation | async-start | bytes 33554432 | tf_op jit(solution)/shard_map/all_to_all | solution.py:74
  22.1 343.3 %copy-start.5 = (f32[5,512]{1,0:T(8,128)S(1)}, f32[5,512]{1,0:T(8,128)}, u32[]{:S(2)}) copy-start(f32[5,512]{1,0:T(8,128)} %param.21) | copy-start | bytes 30724
  22.2 386.4 %all-gather.6.cloned.1.call-start = ((), (), s32[]{:S(2)}) async-start(), calls=%async_computation.1 | async-start | bytes 8912896 | tf_op jit(solution)/shard_map/all_gather | solution.py:76
  26.4 490.2 %all-gather.8.cloned.1.call-start = ((), (), s32[]{:S(2)}) async-start(), calls=%async_computation.2 | async-start | bytes 8912896 | tf_op jit(solution)/shard_map/all_gather | solution.py:21
  408.5 10.3 %copy-start.9 = (f32[2,512]{1,0:T(2,128)S(1)}, f32[2,512]{1,0:T(2,128)}, u32[]{:S(2)}) copy-start(f32[2,512]{1,0:T(2,128)} %param.17) | copy-start | bytes 12292
  418.8 20.5 %copy-start.6 = (bf16[3,512]{1,0:T(4,128)(2,1)S(1)}, bf16[3,512]{1,0:T(4,128)(2,1)}, u32[]{:S(2)}) copy-start(bf16[3,512]{1,0:T(4,128)(2,1)} %param.23) | copy-start | bytes 9220
  433.7 5.6 copy-start.2
  433.8 5.6 collective-permute-start
  516.7 73.6 %copy-start.1 = (bf16[3,8,512]{2,1,0:T(8,128)(2,1)S(1)}, bf16[3,8,512]{2,1,0:T(8,128)(2,1)}, u32[]{:S(2)}) copy-start(bf16[3,8,512]{2,1,0:T(8,128)(2,1)} %param.24) | copy-start | bytes 73732
  516.7 72.4 %copy-start.3 = (bf16[512,2,512]{2,0,1:T(8,128)(2,1)S(1)}, bf16[512,2,512]{2,0,1:T(8,128)(2,1)}, u32[]{:S(2)}) copy-start(bf16[512,2,512]{2,0,1:T(8,128)(2,1)} %copy-done.2) | copy-start | bytes 3145732
  516.7 72.4 %copy-start.7 = (f32[512]{0:T(512)S(1)}, f32[512]{0:T(512)}, u32[]{:S(2)}) copy-start(f32[512]{0:T(512)} %param.27) | copy-start | bytes 6148
Sparse Core Ops, SparseCore 0:
  26.6 258.4 all-gather.5
  442.8 73.7 all-gather.7
